TPU v7x, 32 devices: a whole 2x2x4 slice. The times are simulated.
32 devices in a mesh: pipe: 4 (over y, x), expert: 8 (over z, core).
Axes of the slice: x: 2, y: 2, z: 4, core: 2. Of those that a mesh axis runs over, the one named last changes fastest.
Arguments:
- activations: bfloat16 [4, 1024, 2560], P('pipe', 'expert'), may hold values from -6 to 6
- out_grad: bfloat16 [4, 1024, 2560], P('pipe', 'expert'), may hold values from -6 to 6
- expert_ids: int32 [4, 1024, 2], P('pipe', 'expert'), may hold values from 0 to 3, all different within a row; in each aligned block of 128 rows (0 to 127, 128 to 255, ..., all dimensions but the last counted through in order) at most 96 rows name the same one
- gate_values: float32 [4, 1024, 2], P('pipe', 'expert'), may hold values from 0.1 to 1
- w_gate: bfloat16 [4, 2560, 3072], P('pipe', None, 'expert'), may hold values from -0.125 to 0.125
- w_up: bfloat16 [4, 2560, 3072], P('pipe', None, 'expert'), may hold values from -0.125 to 0.125
- w_down: bfloat16 [4, 3072, 2560], P('pipe', 'expert'), may hold values from -0.21875 to 0.21875
Outputs:
- passed_grad: bfloat16 [4, 1024, 2560], P('pipe', 'expert')
- router_grad: float32 [4, 1024, 2], P('pipe', 'expert')
Inputs may be any that keep to these rules, and one draw needn't show every extreme that they name: `expert_ids`: each row names 2 different experts. In the 128 rows of one section on one device (aligned blocks of rows) no expert is named by more than 96 rows, a bound that some block reaches; every expert is named somewhere.
All inputs are finite; a program needn't handle non-finite values.
Results may differ from a plain program's by a relative error of at most 0.0095.
Values may be sent and summed in bfloat16 or wider, within the bound.
A program may use at most 128 MiB of HBM per device.

v0:
```python
import jax
import jax.numpy as jnp
from jax import lax
from jax.sharding import PartitionSpec as P


def shifted(block, axis, distance):
    devices = range(lax.axis_size(axis))
    route = [(i - distance, i) for i in devices if i - distance in devices]
    return lax.ppermute(block, axis, route)


def expert_terms(rows_in, rows_grad, gate_cols, up_cols, down_rows):
    contract = (((1,), (1,)), ((), ()))
    gate_pre = jnp.dot(rows_in, gate_cols, preferred_element_type=jnp.float32)
    up_pre = jnp.dot(rows_in, up_cols, preferred_element_type=jnp.float32)
    squash = jax.nn.sigmoid(gate_pre)
    activated = gate_pre * squash
    hidden = (activated * up_pre).astype(jnp.bfloat16)
    back_hidden = lax.dot_general(
        rows_grad, down_rows, contract, preferred_element_type=jnp.float32
    )
    router_part = jnp.sum(hidden.astype(jnp.float32) * back_hidden, axis=1)
    slope = squash * (1.0 + gate_pre * (1.0 - squash))
    grad_gate = (back_hidden * up_pre * slope).astype(jnp.bfloat16)
    grad_up = (back_hidden * activated).astype(jnp.bfloat16)
    route_part = lax.dot_general(grad_gate, gate_cols, contract, preferred_element_type=jnp.float32)
    route_part = route_part + lax.dot_general(
        grad_up, up_cols, contract, preferred_element_type=jnp.float32
    )
    return (route_part, router_part)


def local(activations, out_grad, expert_ids, gate_values, w_gate, w_up, w_down):
    inputs = activations[0]
    grads_out = out_grad[0]
    routes = expert_ids[0]
    weights_gate = gate_values[0]
    gate_local = w_gate[0]
    up_local = w_up[0]
    down_local = w_down[0]
    devices_e = lax.axis_size("expert")
    owners = devices_e // 2
    tokens_dev, top_k = routes.shape
    feat_width = inputs.shape[1]
    capacity = min(tokens_dev * 3 // 4, tokens_dev * top_k * 3 // (2 * owners))
    count_entries = tokens_dev * top_k
    flat_ids = routes.reshape(-1)
    one_hot = (flat_ids[:, None] == jnp.arange(owners, dtype=jnp.int32)[None, :]).astype(jnp.int32)
    slot_rank = jnp.sum((jnp.cumsum(one_hot, axis=0) - 1) * one_hot, axis=1)
    slot_index = flat_ids * capacity + slot_rank
    slot_table = (
        jnp.full((owners * capacity,), count_entries, jnp.int32)
        .at[slot_index]
        .set(jnp.arange(count_entries, dtype=jnp.int32))
    )
    token_of = slot_table // top_k
    pad_row = jnp.zeros((1, feat_width), inputs.dtype)
    send_in = jnp.concatenate([inputs, pad_row], 0)[token_of].reshape(owners, capacity, feat_width)
    send_grad = jnp.concatenate([grads_out, pad_row], 0)[token_of].reshape(
        owners, capacity, feat_width
    )
    full_in = lax.all_to_all(
        jnp.repeat(send_in, 2, axis=0), "expert", split_axis=0, concat_axis=0, tiled=True
    )
    item_count = full_in.shape[1]
    route_part, router_part = expert_terms(
        full_in.reshape(-1, feat_width),
        lax.all_to_all(
            jnp.repeat(send_grad, 2, axis=0), "expert", split_axis=0, concat_axis=0, tiled=True
        ).reshape(-1, feat_width),
        gate_local,
        up_local,
        down_local,
    )
    route_part = route_part.reshape(devices_e, item_count, feat_width)
    router_part = router_part.reshape(devices_e, item_count)
    back_route = lax.all_to_all(
        route_part.astype(jnp.bfloat16), "expert", split_axis=0, concat_axis=0, tiled=True
    ).astype(route_part.dtype)
    back_router = lax.all_to_all(
        router_part.astype(jnp.bfloat16), "expert", split_axis=0, concat_axis=0, tiled=True
    ).astype(router_part.dtype)
    summed = jnp.sum(back_route.reshape(owners, 2, item_count, feat_width), axis=1)
    router_sum = jnp.sum(back_router.reshape(owners, 2, item_count), axis=1)
    route_sum, router_sum = (summed, router_sum)
    entry_route = route_sum.reshape(-1, feat_width)[slot_index]
    entry_router = router_sum.reshape(-1)[slot_index]
    input_grad = jnp.sum(
        weights_gate.reshape(tokens_dev, top_k, 1)
        * entry_route.reshape(tokens_dev, top_k, feat_width),
        axis=1,
    ).astype(jnp.bfloat16)
    passed = shifted(input_grad, "pipe", -1)
    return (passed[None], entry_router.reshape(tokens_dev, top_k)[None])


def solution(mesh):
    return jax.shard_map(
        local,
        mesh=mesh,
        in_specs=(
            P("pipe", "expert", None),
            P("pipe", "expert", None),
            P("pipe", "expert", None),
            P("pipe", "expert", None),
            P("pipe", None, "expert"),
            P("pipe", None, "expert"),
            P("pipe", "expert", None),
        ),
        out_specs=(P("pipe", "expert", None), P("pipe", "expert", None)),
        check_vma=False,
    )
```

profile of v0, /device:TPU:0, one launch (start us, length us, event | category | flops | bytes accessed | tf_op | source)
XLA Modules:
  0.0 350.7 jit_solution(5297020244395157370)
XLA Ops:
  0.6 0.0 copy-start
  0.6 0.9 copy.21
  1.6 0.1 eq.29
  1.7 0.1 eq.25
  1.9 0.7 broadcast_multiply_fusion
  2.5 1.2 reduce-window.6
  3.8 0.1 slice.16
  3.8 0.1 copy.23
  4.0 0.1 copy.24
  4.1 0.1 add_bitcast_fusion
  4.1 0.1 copy.20
  4.3 0.1 mul.57
  4.4 1.4 scatter_custom_fusion
  5.9 1.1 concatenate.7
  7.0 3.3 gather_fusion.1
  10.3 3.8 %broadcast_in_dim.24 = bf16[4,2,96,2560]{3,2,1,0:T(8,128)(2,1)} broadcast(bf16[4,96,2560]{2,1,0:T(8,128)(2,1)} %bitcast.56), dimensions={0,2,3} | broadcast | bytes 5898240 | tf_op jit(solution)/shard_map/broadcast_in_dim | solution.py:64
  14.1 0.0 copy-start.4
  14.1 6.5 %all-to-all-start.1 = ((bf16[8,96,2560]{2,1,0:T(8,128)(2,1)}), bf16[8,96,2560]{2,1,0:T(8,128)(2,1)}, u32[]{:S(2)}, u32[]{:S(2)}) async-start(bf16[8,96,2560]{2,1,0:T(8,128)(2,1)} %bitcast.52), calls=%async_computation.1 | async-start | bytes 7864320 | tf_op jit(solution)/shard_map/all_to_all | solution.py:63
  20.6 0.0 copy-done.4
  20.6 3.3 gather_fusion
  23.9 85.1 %all-to-all-done.1 = bf16[8,96,2560]{2,1,0:T(8,128)(2,1)} async-done(((bf16[8,96,2560]{2,1,0:T(8,128)(2,1)}), bf16[8,96,2560]{2,1,0:T(8,128)(2,1)}, u32[]{:S(2)}, u32[]{:S(2)}) %all-to-all-start.1) | async-done | bytes 3932192 | tf_op jit(solution)/shard_map/all_to_all | solution.py:63
  109.0 3.8 %broadcast_in_dim.23 = bf16[4,2,96,2560]{3,2,1,0:T(8,128)(2,1)} broadcast(bf16[4,96,2560]{2,1,0:T(8,128)(2,1)} %bitcast.55), dimensions={0,2,3} | broadcast | bytes 5898240 | tf_op jit(solution)/shard_map/broadcast_in_dim | solution.py:70
  112.8 4.7 %all-to-all-start = ((bf16[8,96,2560]{2,1,0:T(8,128)(2,1)}), bf16[8,96,2560]{2,1,0:T(8,128)(2,1)}, u32[]{:S(2)}, u32[]{:S(2)}) async-start(bf16[8,96,2560]{2,1,0:T(8,128)(2,1)} %bitcast.53), calls=%async_computation | async-start | bytes 7864320 | tf_op jit(solution)/shard_map/all_to_all | solution.py:69
  117.5 0.0 copy-done
  117.6 0.0 copy-start.2
  117.6 4.0 %fusion.2 = f32[768,384]{0,1:T(8,128)S(1)} fusion(bf16[768,2560]{1,0:T(8,128)(2,1)} %bitcast.13, bf16[1,2560,384]{2,1,0:T(8,128)(2,1)S(1)} %copy-done), kind=kOutput, calls=%fused_computation.10 | convolution fusion | flops 1509949440 | bytes 7077888 | tf_op jit(solution)/shard_map/dot_general | solution.py:15
  121.6 0.0 copy-done.2
  121.6 4.9 %fusion.5 = f32[768,384]{0,1:T(8,128)} fusion(bf16[768,2560]{1,0:T(8,128)(2,1)} %bitcast.13, bf16[1,2560,384]{2,1,0:T(8,128)(2,1)S(1)} %copy-done.2), kind=kOutput, calls=%fused_computation.13 | convolution fusion | flops 1509949440 | bytes 7077888 | tf_op jit(solution)/shard_map/dot_general | solution.py:16
  126.5 79.3 %all-to-all-done = bf16[8,96,2560]{2,1,0:T(8,128)(2,1)} async-done(((bf16[8,96,2560]{2,1,0:T(8,128)(2,1)}), bf16[8,96,2560]{2,1,0:T(8,128)(2,1)}, u32[]{:S(2)}, u32[]{:S(2)}) %all-to-all-start) | async-done | bytes 3932192 | tf_op jit(solution)/shard_map/all_to_all | solution.py:69
  205.7 0.0 copy-start.1
  205.7 4.9 %multiply_reduce_fusion.1 = (bf16[768]{0:T(1024)(128)(2,1)S(1)}, f32[768,384]{0,1:T(8,128)S(1)}) fusion(f32[768,384]{0,1:T(8,128)} %fusion.5, f32[768,384]{0,1:T(8,128)S(1)} %fusion.2, bf16[768,2560]{1,0:T(8,128)(2,1)} %bitcast.8, bf16[1,384,2560]{2,1,0:T(8,128)(2,1)} %param.13), kind=kOutput, calls=%fused_computation.17 | convolution fusion | flops 1512602880 | bytes 9438720 | tf_op jit(solution)/shard_map/dot_general | solution.py:20
  210.6 0.0 copy-done.1
  210.7 0.0 copy-start.3
  210.7 2.5 fusion
  213.1 0.0 copy-done.3
  213.1 4.3 %add_convert_fusion = bf16[768,2560]{1,0:T(8,128)(2,1)} fusion(f32[768,2560]{1,0:T(8,128)S(1)} %fusion, bf16[1,2560,384]{2,1,0:T(8,128)(2,1)S(1)} %copy-done.3, f32[768,384]{0,1:T(8,128)S(1)} %get-tuple-element.7, f32[768,384]{0,1:T(8,128)S(1)} %fusion.2), kind=kOutput, calls=%fused_computation.6 | convolution fusion | flops 1515651072 | bytes 16121856 | tf_op jit(solution)/shard_map/dot_general | solution.py:28
  217.4 0.0 copy-start.5
  217.4 4.9 %all-to-all-start.2 = ((bf16[8,96,2560]{2,1,0:T(8,128)(2,1)}), bf16[8,96,2560]{2,1,0:T(8,128)(2,1)}, u32[]{:S(2)}, u32[]{:S(2)}) async-start(bf16[8,96,2560]{2,1,0:T(8,128)(2,1)} %bitcast.54), calls=%async_computation.2 | async-start | bytes 7864320 | tf_op jit(solution)/shard_map/all_to_all | solution.py:78
  222.3 0.0 copy-done.5
  222.3 0.1 copy.19
  222.4 88.0 %all-to-all-done.2 = bf16[8,96,2560]{2,1,0:T(8,128)(2,1)} async-done(((bf16[8,96,2560]{2,1,0:T(8,128)(2,1)}), bf16[8,96,2560]{2,1,0:T(8,128)(2,1)}, u32[]{:S(2)}, u32[]{:S(2)}) %all-to-all-start.2) | async-done | bytes 3932192 | tf_op jit(solution)/shard_map/all_to_all | solution.py:78
  310.4 5.2 %convert_reduce_fusion = f32[4,96,2560]{2,1,0:T(8,128)} fusion(bf16[8,96,2560]{2,1,0:T(8,128)(2,1)} %all-to-all-done.2), kind=kLoop, calls=%fused_computation.5 | loop fusion | flops 2949120 | bytes 7864320 | tf_op jit(solution)/shard_map/reduce_sum | solution.py:84
  315.7 6.2 %gather_fusion.2 = f32[256,2560]{1,0:T(8,128)} fusion(f32[384,2560]{1,0:T(8,128)} %bitcast.51, s32[1024]{0:T(1024)S(1)} %pad_clamp_fusion), kind=kCustom, calls=%fused_computation.2 | custom fusion | bytes 5243904 | tf_op jit(solution)/shard_map/gather | solution.py:87
  321.9 4.4 %reshape.115 = f32[128,2,2560]{2,1,0:T(2,128)} reshape(f32[256,2560]{1,0:T(8,128)} %gather_fusion.2) | data formatting | bytes 5242880 | tf_op jit(solution)/shard_map/reshape | solution.py:91
  326.3 5.5 %multiply_reduce_fusion = bf16[128,2560]{1,0:T(8,128)(2,1)S(1)} fusion(f32[128,2,2560]{2,1,0:T(2,128)} %reshape.115, f32[128,2]{1,0:T(8,128)S(1)} %copy.19), kind=kLoop, calls=%fused_computation.7 | loop fusion | flops 983040 | bytes 3277824 | tf_op jit(solution)/shard_map/reduce_sum | solution.py:89
  331.8 1.3 collective-permute-start
  333.1 0.1 convert_element_type.64
  333.2 7.9 %all_to_all.21 = bf16[8,1,96]{2,1,0:T(2,128)(2,1)S(1)} all-to-all(bf16[8,1,96]{2,1,0:T(2,128)(2,1)S(1)} %convert_element_type.64), channel_id=1, replica_groups=mesh['pipe'=4,'expert'=8] {'expert'}, dimensions={0} | all-to-all | bytes 3072 | tf_op jit(solution)/shard_map/all_to_all | solution.py:81
  341.1 0.1 reshape.116
  341.2 1.9 gather_fusion.3
  343.2 0.1 broadcast_in_dim_reshape.3
  343.3 0.6 copy.26
  344.0 5.9 %collective-permute-done = bf16[128,2560]{1,0:T(8,128)(2,1)S(1)} collective-permute-done((bf16[128,2560]{1,0:T(8,128)(2,1)S(1)}, bf16[128,2560]{1,0:T(8,128)(2,1)S(1)}, u32[]{:S(2)}, u32[]{:S(2)}) %collective-permute-start) | collective-permute-done | bytes 655392 | tf_op jit(solution)/shard_map/ppermute | solution.py:10
  349.9 0.8 copy.30
  (12 shorter events, 0.2 us)
Async XLA Ops:
  0.6 116.9 %copy-start = (bf16[1,2560,384]{2,1,0:T(8,128)(2,1)S(1)}, bf16[1,2560,384]{2,1,0:T(8,128)(2,1)}, u32[]{:S(2)}) copy-start(bf16[1,2560,384]{2,1,0:T(8,128)(2,1)} %param.11) | copy-start | bytes 5898244
  14.1 6.5 %copy-start.4 = (bf16[1,128,2560]{2,1,0:T(8,128)(2,1)S(1)}, bf16[1,128,2560]{2,1,0:T(8,128)(2,1)}, u32[]{:S(2)}) copy-start(bf16[1,128,2560]{2,1,0:T(8,128)(2,1)} %param.8) | copy-start | bytes 1966084
  14.1 94.9 %all-to-all-start.1 = ((bf16[8,96,2560]{2,1,0:T(8,128)(2,1)}), bf16[8,96,2560]{2,1,0:T(8,128)(2,1)}, u32[]{:S(2)}, u32[]{:S(2)}) async-start(bf16[8,96,2560]{2,1,0:T(8,128)(2,1)} %bitcast.52), calls=%async_computation.1 | async-start | bytes 7864320 | tf_op jit(solution)/shard_map/all_to_all | solution.py:63
  112.8 92.9 %all-to-all-start = ((bf16[8,96,2560]{2,1,0:T(8,128)(2,1)}), bf16[8,96,2560]{2,1,0:T(8,128)(2,1)}, u32[]{:S(2)}, u32[]{:S(2)}) async-start(bf16[8,96,2560]{2,1,0:T(8,128)(2,1)} %bitcast.53), calls=%async_computation | async-start | bytes 7864320 | tf_op jit(solution)/shard_map/all_to_all | solution.py:69
  117.6 4.0 %copy-start.2 = (bf16[1,2560,384]{2,1,0:T(8,128)(2,1)S(1)}, bf16[1,2560,384]{2,1,0:T(8,128)(2,1)}, u32[]{:S(2)}) copy-start(bf16[1,2560,384]{2,1,0:T(8,128)(2,1)} %param.12) | copy-start | bytes 5898244
  205.7 4.9 %copy-start.1 = (f32[768,384]{0,1:T(8,128)S(1)}, f32[768,384]{0,1:T(8,128)}, u32[]{:S(2)}) copy-start(f32[768,384]{0,1:T(8,128)} %fusion.5) | copy-start | bytes 3538948
  210.7 2.5 copy-start.3
  217.4 4.9 %copy-start.5 = (f32[1,128,2]{1,2,0:T(2,128)S(1)}, f32[1,128,2]{1,2,0:T(2,128)}, u32[]{:S(2)}) copy-start(f32[1,128,2]{1,2,0:T(2,128)} %param.10) | copy-start | bytes 3076
  217.4 93.0 %all-to-all-start.2 = ((bf16[8,96,2560]{2,1,0:T(8,128)(2,1)}), bf16[8,96,2560]{2,1,0:T(8,128)(2,1)}, u32[]{:S(2)}, u32[]{:S(2)}) async-start(bf16[8,96,2560]{2,1,0:T(8,128)(2,1)} %bitcast.54), calls=%async_computation.2 | async-start | bytes 7864320 | tf_op jit(solution)/shard_map/all_to_all | solution.py:78
  331.8 18.1 %collective-permute-start = (bf16[128,2560]{1,0:T(8,128)(2,1)S(1)}, bf16[128,2560]{1,0:T(8,128)(2,1)S(1)}, u32[]{:S(2)}, u32[]{:S(2)}) collective-permute-start(bf16[128,2560]{1,0:T(8,128)(2,1)S(1)} %multiply_reduce_fusion), channel_id=1, source_target_pairs={{8,0},{16,8},{24,16},{9,1},{17,9},{25,17},{10,2},{18,10},{26,18},{... | collective-permute-start | bytes 1966088 | tf_op jit(solution)/shard_map/ppermute | solution.py:10
where the time goes:
time: 351 us
  waiting for transfers between devices  258 us (74%)
  local copies, waits for them, and re-layouts  32.9 us (9%)
  matrix products  20.5 us (6%)
  starting transfers between devices  17.4 us (5%)
  other arithmetic  12.8 us (4%)
  blocking collectives  7.94 us (2%)
    all_to_all x1, waiting for transfers between devices, local(): lax.all_to_all(route_part.astype(jnp.bfloat16), 'expert', split_axis=0, c...  88 us
    all_to_all x1, waiting for transfers between devices, local(): lax.all_to_all(jnp.repeat(send_in, 2, axis=0), 'expert', split_axis=0, co...  85.1 us
    all_to_all x1, waiting for transfers between devices, local(): lax.all_to_all(jnp.repeat(send_grad, 2, axis=0), 'expert', split_axis=0,...  79.3 us
    all_to_all x1, blocking collectives, local(): lax.all_to_all(router_part.astype(jnp.bfloat16), 'expert', split_axis=0,...  7.94 us
  transfers between devices with their start and end apart: 4, of which 4 were waited for; matrix products, arithmetic and copies ran while one was open for 4% of the time, Pallas kernels for 0%

commit v1 on v0

--- a/solution.py
+++ b/solution.py
@@ -2,6 +2,22 @@
 import jax.numpy as jnp
 from jax import lax
 from jax.sharding import PartitionSpec as P
+
+
+def swapped_with_each(x, axis, split, join):
+    ways, here = (lax.axis_size(axis), lax.axis_index(axis))
+    width = x.shape[split] // ways
+    dims = list(x.shape)
+    dims[split] = width
+    height = dims[join]
+    dims[join] = height * ways
+    full = jnp.zeros(dims, x.dtype)
+    for mask in range(ways):
+        part = lax.dynamic_slice_in_dim(x, (here ^ mask) * width, width, axis=split)
+        if mask:
+            part = lax.ppermute(part, axis, [(d, d ^ mask) for d in range(ways)])
+        full = lax.dynamic_update_slice_in_dim(full, part, (here ^ mask) * height, axis=join)
+    return full
 
 
 def shifted(block, axis, distance):
@@ -60,9 +76,7 @@
     send_grad = jnp.concatenate([grads_out, pad_row], 0)[token_of].reshape(
         owners, capacity, feat_width
     )
-    full_in = lax.all_to_all(
-        jnp.repeat(send_in, 2, axis=0), "expert", split_axis=0, concat_axis=0, tiled=True
-    )
+    full_in = swapped_with_each(jnp.repeat(send_in, 2, axis=0), "expert", 0, 0)
     item_count = full_in.shape[1]
     route_part, router_part = expert_terms(
         full_in.reshape(-1, feat_width),

time: 351 us -> 341 us (0.972)
  waiting for transfers between devices: 258 us -> 229 us
  starting transfers between devices: 17.4 us -> 41.9 us
  matrix products: 20.5 us -> 16.2 us
    ppermute x0 -> x7, waiting for transfers between devices: none -> 134 us  [swapped_with_each(): part = lax.ppermute(part, axis, [(d, d ^ mask) for d in range(ways)])]
    all_to_all x1 -> x0, waiting for transfers between devices: 85.1 us -> none  [local(): lax.all_to_all(jnp.repeat(send_in, 2, axis=0), 'expert', split_axis=0, co...]
    all_to_all x1, waiting for transfers between devices: 79.3 us -> 0.01 us  [local(): lax.all_to_all(jnp.repeat(send_grad, 2, axis=0), 'expert', split_axis=0,...]
    all_to_all x1, starting transfers between devices: 4.86 us -> 23.3 us  [local(): lax.all_to_all(route_part.astype(jnp.bfloat16), 'expert', split_axis=0, c...]
    ppermute x0 -> x7, starting transfers between devices: none -> 10.8 us  [swapped_with_each(): part = lax.ppermute(part, axis, [(d, d ^ mask) for d in range(ways)])]
    all_to_all x1 -> x0, starting transfers between devices: 6.49 us -> none  [local(): lax.all_to_all(jnp.repeat(send_in, 2, axis=0), 'expert', split_axis=0, co...]
  transfers between devices with their start and end apart: 4 -> 10, of which waited for: 4 -> 6; matrix products, arithmetic and copies ran while one was open for 4% -> 4% of each run, Pallas kernels for 0% -> 0%
where the time goes in v1:
time: 341 us; the launch traced here: 340 us
  waiting for transfers between devices  229 us (67%)
  starting transfers between devices  41.9 us (12%)
  local copies, waits for them, and re-layouts  32 us (9%)
  matrix products  16.2 us (5%)
  other arithmetic  12.8 us (4%)
  blocking collectives  7.94 us (2%)
    ppermute x7, waiting for transfers between devices, swapped_with_each(): part = lax.ppermute(part, axis, [(d, d ^ mask) for d in range(ways)])  134 us
    all_to_all x1, waiting for transfers between devices, local(): lax.all_to_all(route_part.astype(jnp.bfloat16), 'expert', split_axis=0, c...  88.8 us
    all_to_all x1, starting transfers between devices, local(): lax.all_to_all(route_part.astype(jnp.bfloat16), 'expert', split_axis=0, c...  23.3 us
    ppermute x7, starting transfers between devices, swapped_with_each(): part = lax.ppermute(part, axis, [(d, d ^ mask) for d in range(ways)])  10.8 us
    all_to_all x1, blocking collectives, local(): lax.all_to_all(router_part.astype(jnp.bfloat16), 'expert', split_axis=0,...  7.94 us
  transfers between devices with their start and end apart: 10, of which 6 were waited for; matrix products, arithmetic and copies ran while one was open for 4% of the time, Pallas kernels for 0%

profile of v1, /device:TPU:0, one launch (start us, length us, event | category | flops | bytes accessed | tf_op | source)
XLA Modules:
  0.0 340.5 jit_solution(13140686146567877030)
XLA Ops:
  0.6 0.0 copy-start
  0.6 0.9 copy.21
  1.6 0.1 eq.29
  1.7 0.1 eq.25
  1.9 0.7 broadcast_multiply_fusion
  2.5 1.2 reduce-window.6
  3.8 0.1 slice.16
  3.8 0.1 copy.23
  4.0 0.1 copy.24
  4.1 0.1 add_bitcast_fusion
  4.1 0.1 copy.20
  4.3 0.1 mul.57
  4.4 1.4 scatter_custom_fusion
  5.9 1.1 concatenate.6
  7.0 3.3 gather_fusion
  10.3 3.8 %broadcast_in_dim.26 = bf16[4,2,96,2560]{3,2,1,0:T(8,128)(2,1)} broadcast(bf16[4,96,2560]{2,1,0:T(8,128)(2,1)} %bitcast.56), dimensions={0,2,3} | broadcast | bytes 5898240 | tf_op jit(solution)/shard_map/broadcast_in_dim | solution.py:84
  14.1 6.5 %all-to-all-start = ((bf16[8,96,2560]{2,1,0:T(8,128)(2,1)}), bf16[8,96,2560]{2,1,0:T(8,128)(2,1)}, u32[]{:S(2)}, u32[]{:S(2)}) async-start(bf16[8,96,2560]{2,1,0:T(8,128)(2,1)} %bitcast.53), calls=%async_computation | async-start | bytes 7864320 | tf_op jit(solution)/shard_map/all_to_all | solution.py:83
  20.5 0.0 copy-done.4
  20.6 3.3 gather_fusion.1
  23.9 1.9 broadcast_in_dim.28
  25.8 0.3 broadcast_in_dim.27
  26.1 0.4 constant_dynamic-slice_fusion
  26.5 0.6 collective-permute-start
  27.1 1.6 collective-permute-start.1
  28.7 0.0 collective-permute-start.2
  28.7 2.6 collective-permute-start.3
  31.4 0.1 collective-permute-start.4
  31.5 0.0 collective-permute-done
  31.5 3.4 %collective-permute-start.5 = (bf16[1,96,2560]{2,1,0:T(8,128)(2,1)S(1)}, bf16[1,96,2560]{2,1,0:T(8,128)(2,1)S(1)}, u32[]{:S(2)}, u32[]{:S(2)}) collective-permute-start(bf16[1,96,2560]{2,1,0:T(8,128)(2,1)S(1)} %get-tuple-element.7), channel_id=1, source_target_pairs={{0,6},{1,7},{2,4},{3,5},{4,2},{5,3},{6,0},{7,1},{8,14},{9,15},{10,... | collective-permute-start | bytes 1474568 | tf_op jit(solution)/shard_map/ppermute | solution.py:18
  35.0 60.7 %collective-permute-done.1 = bf16[1,96,2560]{2,1,0:T(8,128)(2,1)S(1)} collective-permute-done((bf16[1,96,2560]{2,1,0:T(8,128)(2,1)S(1)}, bf16[1,96,2560]{2,1,0:T(8,128)(2,1)S(1)}, u32[]{:S(2)}, u32[]{:S(2)}) %collective-permute-start.1) | collective-permute-done | bytes 491552 | tf_op jit(solution)/shard_map/ppermute | solution.py:18
  95.6 2.4 collective-permute-start.6
  98.1 8.0 %collective-permute-done.2 = bf16[1,96,2560]{2,1,0:T(8,128)(2,1)S(1)} collective-permute-done((bf16[1,96,2560]{2,1,0:T(8,128)(2,1)S(1)}, bf16[1,96,2560]{2,1,0:T(8,128)(2,1)S(1)}, u32[]{:S(2)}, u32[]{:S(2)}) %collective-permute-start.2) | collective-permute-done | bytes 491552 | tf_op jit(solution)/shard_map/ppermute | solution.py:18
  106.2 56.0 %collective-permute-done.3 = bf16[1,96,2560]{2,1,0:T(8,128)(2,1)S(1)} collective-permute-done((bf16[1,96,2560]{2,1,0:T(8,128)(2,1)S(1)}, bf16[1,96,2560]{2,1,0:T(8,128)(2,1)S(1)}, u32[]{:S(2)}, u32[]{:S(2)}) %collective-permute-start.3) | collective-permute-done | bytes 491552 | tf_op jit(solution)/shard_map/ppermute | solution.py:18
  162.2 9.3 %collective-permute-done.4 = bf16[1,96,2560]{2,1,0:T(8,128)(2,1)S(1)} collective-permute-done((bf16[1,96,2560]{2,1,0:T(8,128)(2,1)S(1)}, bf16[1,96,2560]{2,1,0:T(8,128)(2,1)S(1)}, u32[]{:S(2)}, u32[]{:S(2)}) %collective-permute-start.4) | collective-permute-done | bytes 491552 | tf_op jit(solution)/shard_map/ppermute | solution.py:18
  171.6 0.0 collective-permute-done.5
  171.6 0.0 collective-permute-done.6
  171.7 0.0 copy-done
  171.7 0.0 copy-start.2
  171.7 1.7 fusion.2
  173.4 0.0 copy-done.2
  173.5 2.9 fusion.5
  176.3 0.0 all-to-all-done
  176.3 4.9 %multiply_reduce_fusion.1 = (bf16[768]{0:T(1024)(128)(2,1)S(1)}, f32[768,384]{0,1:T(8,128)S(1)}) fusion(f32[768,384]{0,1:T(8,128)} %fusion.5, f32[768,384]{0,1:T(8,128)S(1)} %fusion.2, bf16[768,2560]{1,0:T(8,128)(2,1)} %bitcast.8, bf16[1,384,2560]{2,1,0:T(8,128)(2,1)} %param.13), kind=kOutput, calls=%fused_computation.17 | convolution fusion | flops 1512602880 | bytes 9438720 | tf_op jit(solution)/shard_map/dot_general | solution.py:36
  181.2 0.0 copy-done.1
  181.2 0.0 copy-start.3
  181.3 2.5 fusion
  183.7 0.0 copy-done.3
  183.7 4.3 %add_convert_fusion = bf16[768,2560]{1,0:T(8,128)(2,1)} fusion(f32[768,2560]{1,0:T(8,128)S(1)} %fusion, bf16[1,2560,384]{2,1,0:T(8,128)(2,1)S(1)} %copy-done.3, f32[768,384]{0,1:T(8,128)S(1)} %get-tuple-element.15, f32[768,384]{0,1:T(8,128)S(1)} %fusion.2), kind=kOutput, calls=%fused_computation.6 | convolution fusion | flops 1515651072 | bytes 16121856 | tf_op jit(solution)/shard_map/dot_general | solution.py:44
  188.0 23.3 %all-to-all-start.1 = ((bf16[8,96,2560]{2,1,0:T(8,128)(2,1)}), bf16[8,96,2560]{2,1,0:T(8,128)(2,1)}, u32[]{:S(2)}, u32[]{:S(2)}) async-start(bf16[8,96,2560]{2,1,0:T(8,128)(2,1)} %bitcast.54), calls=%async_computation.1 | async-start | bytes 7864320 | tf_op jit(solution)/shard_map/all_to_all | solution.py:92
  211.3 0.1 copy.19
  211.5 88.8 %all-to-all-done.1 = bf16[8,96,2560]{2,1,0:T(8,128)(2,1)} async-done(((bf16[8,96,2560]{2,1,0:T(8,128)(2,1)}), bf16[8,96,2560]{2,1,0:T(8,128)(2,1)}, u32[]{:S(2)}, u32[]{:S(2)}) %all-to-all-start.1) | async-done | bytes 3932192 | tf_op jit(solution)/shard_map/all_to_all | solution.py:92
  300.2 5.2 %convert_reduce_fusion = f32[4,96,2560]{2,1,0:T(8,128)} fusion(bf16[8,96,2560]{2,1,0:T(8,128)(2,1)} %all-to-all-done.1), kind=kLoop, calls=%fused_computation.5 | loop fusion | flops 2949120 | bytes 7864320 | tf_op jit(solution)/shard_map/reduce_sum | solution.py:98
  305.5 6.2 %gather_fusion.2 = f32[256,2560]{1,0:T(8,128)} fusion(f32[384,2560]{1,0:T(8,128)} %bitcast.51, s32[1024]{0:T(1024)S(1)} %pad_clamp_fusion), kind=kCustom, calls=%fused_computation.2 | custom fusion | bytes 5243904 | tf_op jit(solution)/shard_map/gather | solution.py:101
  311.7 4.4 %reshape.115 = f32[128,2,2560]{2,1,0:T(2,128)} reshape(f32[256,2560]{1,0:T(8,128)} %gather_fusion.2) | data formatting | bytes 5242880 | tf_op jit(solution)/shard_map/reshape | solution.py:105
  316.1 5.5 %multiply_reduce_fusion = bf16[128,2560]{1,0:T(8,128)(2,1)S(1)} fusion(f32[128,2,2560]{2,1,0:T(2,128)} %reshape.115, f32[128,2]{1,0:T(8,128)S(1)} %copy.19), kind=kLoop, calls=%fused_computation.7 | loop fusion | flops 983040 | bytes 3277824 | tf_op jit(solution)/shard_map/reduce_sum | solution.py:103
  321.6 1.3 collective-permute-start.7
  322.9 0.1 convert_element_type.64
  323.0 7.9 %all_to_all.16 = bf16[8,1,96]{2,1,0:T(2,128)(2,1)S(1)} all-to-all(bf16[8,1,96]{2,1,0:T(2,128)(2,1)S(1)} %convert_element_type.64), channel_id=1, replica_groups=mesh['pipe'=4,'expert'=8] {'expert'}, dimensions={0} | all-to-all | bytes 3072 | tf_op jit(solution)/shard_map/all_to_all | solution.py:95
  330.9 0.1 reshape.116
  331.0 1.9 gather_fusion.3
  333.0 0.1 broadcast_in_dim_reshape.3
  333.1 0.6 copy.26
  333.8 5.9 %collective-permute-done.7 = bf16[128,2560]{1,0:T(8,128)(2,1)S(1)} collective-permute-done((bf16[128,2560]{1,0:T(8,128)(2,1)S(1)}, bf16[128,2560]{1,0:T(8,128)(2,1)S(1)}, u32[]{:S(2)}, u32[]{:S(2)}) %collective-permute-start.7) | collective-permute-done | bytes 655392 | tf_op jit(solution)/shard_map/ppermute | solution.py:26
  339.7 0.8 copy.38
  (23 shorter events, 0.4 us)
Async XLA Ops:
  0.6 171.1 %copy-start = (bf16[1,2560,384]{2,1,0:T(8,128)(2,1)S(1)}, bf16[1,2560,384]{2,1,0:T(8,128)(2,1)}, u32[]{:S(2)}) copy-start(bf16[1,2560,384]{2,1,0:T(8,128)(2,1)} %param.11) | copy-start | bytes 5898244
  14.1 6.5 %copy-start.4 = (bf16[1,128,2560]{2,1,0:T(8,128)(2,1)S(1)}, bf16[1,128,2560]{2,1,0:T(8,128)(2,1)}, u32[]{:S(2)}) copy-start(bf16[1,128,2560]{2,1,0:T(8,128)(2,1)} %param.7) | copy-start | bytes 1966084
  14.1 162.3 %all-to-all-start = ((bf16[8,96,2560]{2,1,0:T(8,128)(2,1)}), bf16[8,96,2560]{2,1,0:T(8,128)(2,1)}, u32[]{:S(2)}, u32[]{:S(2)}) async-start(bf16[8,96,2560]{2,1,0:T(8,128)(2,1)} %bitcast.53), calls=%async_computation | async-start | bytes 7864320 | tf_op jit(solution)/shard_map/all_to_all | solution.py:83
  26.5 5.0 %collective-permute-start = (bf16[1,96,2560]{2,1,0:T(8,128)(2,1)S(1)}, bf16[1,96,2560]{2,1,0:T(8,128)(2,1)S(1)}, u32[]{:S(2)}, u32[]{:S(2)}) collective-permute-start(bf16[1,96,2560]{2,1,0:T(8,128)(2,1)S(1)} %get-tuple-element.12), channel_id=1, source_target_pairs={{0,1},{1,0},{2,3},{3,2},{4,5},{5,4},{6,7},{7,6},{8,9},{9,8},{10,11... | collective-permute-start | bytes 1474568 | tf_op jit(solution)/shard_map/ppermute | solution.py:18
  27.1 68.5 %collective-permute-start.1 = (bf16[1,96,2560]{2,1,0:T(8,128)(2,1)S(1)}, bf16[1,96,2560]{2,1,0:T(8,128)(2,1)S(1)}, u32[]{:S(2)}, u32[]{:S(2)}) collective-permute-start(bf16[1,96,2560]{2,1,0:T(8,128)(2,1)S(1)} %get-tuple-element.11), channel_id=1, source_target_pairs={{0,2},{1,3},{2,0},{3,1},{4,6},{5,7},{6,4},{7,5},{8,10},{9,11},{10,... | collective-permute-start | bytes 1474568 | tf_op jit(solution)/shard_map/ppermute | solution.py:18
  28.7 77.4 %collective-permute-start.2 = (bf16[1,96,2560]{2,1,0:T(8,128)(2,1)S(1)}, bf16[1,96,2560]{2,1,0:T(8,128)(2,1)S(1)}, u32[]{:S(2)}, u32[]{:S(2)}) collective-permute-start(bf16[1,96,2560]{2,1,0:T(8,128)(2,1)S(1)} %get-tuple-element.10), channel_id=1, source_target_pairs={{0,3},{1,2},{2,1},{3,0},{4,7},{5,6},{6,5},{7,4},{8,11},{9,10},{10,... | collective-permute-start | bytes 1474568 | tf_op jit(solution)/shard_map/ppermute | solution.py:18
  28.7 133.4 %collective-permute-start.3 = (bf16[1,96,2560]{2,1,0:T(8,128)(2,1)S(1)}, bf16[1,96,2560]{2,1,0:T(8,128)(2,1)S(1)}, u32[]{:S(2)}, u32[]{:S(2)}) collective-permute-start(bf16[1,96,2560]{2,1,0:T(8,128)(2,1)S(1)} %get-tuple-element.9), channel_id=1, source_target_pairs={{0,4},{1,5},{2,6},{3,7},{4,0},{5,1},{6,2},{7,3},{8,12},{9,13},{10,... | collective-permute-start | bytes 1474568 | tf_op jit(solution)/shard_map/ppermute | solution.py:18
  31.4 140.2 %collective-permute-start.4 = (bf16[1,96,2560]{2,1,0:T(8,128)(2,1)S(1)}, bf16[1,96,2560]{2,1,0:T(8,128)(2,1)S(1)}, u32[]{:S(2)}, u32[]{:S(2)}) collective-permute-start(bf16[1,96,2560]{2,1,0:T(8,128)(2,1)S(1)} %get-tuple-element.8), channel_id=1, source_target_pairs={{0,5},{1,4},{2,7},{3,6},{4,1},{5,0},{6,3},{7,2},{8,13},{9,12},{10,... | collective-permute-start | bytes 1474568 | tf_op jit(solution)/shard_map/ppermute | solution.py:18
  31.5 140.1 %collective-permute-start.5 = (bf16[1,96,2560]{2,1,0:T(8,128)(2,1)S(1)}, bf16[1,96,2560]{2,1,0:T(8,128)(2,1)S(1)}, u32[]{:S(2)}, u32[]{:S(2)}) collective-permute-start(bf16[1,96,2560]{2,1,0:T(8,128)(2,1)S(1)} %get-tuple-element.7), channel_id=1, source_target_pairs={{0,6},{1,7},{2,4},{3,5},{4,2},{5,3},{6,0},{7,1},{8,14},{9,15},{10,... | collective-permute-start | bytes 1474568 | tf_op jit(solution)/shard_map/ppermute | solution.py:18
  95.6 76.0 %collective-permute-start.6 = (bf16[1,96,2560]{2,1,0:T(8,128)(2,1)S(1)}, bf16[1,96,2560]{2,1,0:T(8,128)(2,1)S(1)}, u32[]{:S(2)}, u32[]{:S(2)}) collective-permute-start(bf16[1,96,2560]{2,1,0:T(8,128)(2,1)S(1)} %get-tuple-element.6), channel_id=1, source_target_pairs={{0,7},{1,6},{2,5},{3,4},{4,3},{5,2},{6,1},{7,0},{8,15},{9,14},{10,... | collective-permute-start | bytes 1474568 | tf_op jit(solution)/shard_map/ppermute | solution.py:18
  171.7 1.8 copy-start.2
  176.3 4.9 %copy-start.1 = (f32[768,384]{0,1:T(8,128)S(1)}, f32[768,384]{0,1:T(8,128)}, u32[]{:S(2)}) copy-start(f32[768,384]{0,1:T(8,128)} %fusion.5) | copy-start | bytes 3538948
  181.2 2.5 copy-start.3
  188.0 23.3 %copy-start.5 = (f32[1,128,2]{1,2,0:T(2,128)S(1)}, f32[1,128,2]{1,2,0:T(2,128)}, u32[]{:S(2)}) copy-start(f32[1,128,2]{1,2,0:T(2,128)} %param.10) | copy-start | bytes 3076
  188.0 112.2 %all-to-all-start.1 = ((bf16[8,96,2560]{2,1,0:T(8,128)(2,1)}), bf16[8,96,2560]{2,1,0:T(8,128)(2,1)}, u32[]{:S(2)}, u32[]{:S(2)}) async-start(bf16[8,96,2560]{2,1,0:T(8,128)(2,1)} %bitcast.54), calls=%async_computation.1 | async-start | bytes 7864320 | tf_op jit(solution)/shard_map/all_to_all | solution.py:92
  321.6 18.1 %collective-permute-start.7 = (bf16[128,2560]{1,0:T(8,128)(2,1)S(1)}, bf16[128,2560]{1,0:T(8,128)(2,1)S(1)}, u32[]{:S(2)}, u32[]{:S(2)}) collective-permute-start(bf16[128,2560]{1,0:T(8,128)(2,1)S(1)} %multiply_reduce_fusion), channel_id=1, source_target_pairs={{8,0},{16,8},{24,16},{9,1},{17,9},{25,17},{10,2},{18,10},{26,18},{... | collective-permute-start | bytes 1966088 | tf_op jit(solution)/shard_map/ppermute | solution.py:26
